TPU v7x, 128 devices: a whole 4x4x4 slice. The times are simulated.
128 devices in a mesh: tm: 64 (over x, z, y), head: 2 (over core).
Axes of the slice: x: 4, y: 4, z: 4, core: 2. Of those that a mesh axis runs over, the one named last changes fastest.
Arguments:
- series: bfloat16 [16, 65536, 512], P(None, 'tm'), may hold values from -6 to 6
- modes: int32 [128], replicated, may hold values from 1 to 32767, as said below
- query_weight: bfloat16 [512, 512], P(None, 'head'), may hold values from -0.25 to 0.25
- mix_weight: float32 [128, 8, 64, 128], P('tm', 'head'), may hold values from -0.5 to 0.5
- out_weight: bfloat16 [512, 512], P(None, 'head'), may hold values from -0.25 to 0.25
Outputs:
- output: bfloat16 [16, 65536, 512], P(None, 'tm', 'head')
Inputs may be any that keep to these rules, and one draw needn't show every extreme that they name: `modes`: distinct mode numbers; both 1 and one less than half of 65536 are among them.
All inputs are finite; a program needn't handle non-finite values.
Results may differ from a plain program's by a relative error of at most 0.0075.
Values may be sent and summed in bfloat16 or wider, within the bound.
A program may use at most 128 MiB of HBM per device.

v0:
```python
import math
import jax
import jax.numpy as jnp
from jax import lax
from jax.sharding import PartitionSpec as P

two_pi = 2.0 * math.pi


def wave_table(mode_list, first_time, time_count, series_length):
    time_index = first_time + lax.iota(jnp.int32, time_count)
    phases = time_index[:, None] * mode_list[None, :] % series_length
    angles = phases.astype(jnp.float32) * (two_pi / series_length)
    waves = jnp.stack([jnp.cos(angles), -jnp.sin(angles)], axis=2)
    return waves.astype(jnp.bfloat16).reshape(time_count, -1)


def body(series, modes, query_weight, mix_weight, out_weight):
    series_count, shard_rows, model_width = series.shape
    group_width = query_weight.shape[1]
    mode_total = modes.shape[0]
    own_modes, heads_here, head_size, _ = mix_weight.shape
    head_groups = lax.axis_size("head")
    own_series = series_count // head_groups
    series_length = lax.axis_size("tm") * shard_rows
    first_time = lax.axis_index("tm") * shard_rows
    forward_scale = 1.0 / math.sqrt(series_length)
    inverse_scale = 1.0 / math.sqrt(mode_total)
    highest = lax.Precision.HIGHEST
    mine = lax.dynamic_slice_in_dim(series, lax.axis_index("head") * own_series, own_series, 0)
    table = wave_table(modes, first_time, shard_rows, series_length)
    partial = jnp.einsum("tk,btd->kbd", table, mine, preferred_element_type=jnp.float32)
    summed = lax.psum_scatter(partial * forward_scale, "tm", scatter_dimension=0, tiled=True)
    summed = lax.all_gather(summed, "head", axis=1, tiled=True)
    spectrum = jnp.einsum(
        "kbd,df->kbf", summed, query_weight.astype(jnp.float32), precision=highest
    )
    parts = spectrum.reshape(own_modes, 2, series_count, heads_here, head_size)
    from_real = jnp.einsum("mbhi,mhio->mbho", parts[:, 0], mix_weight, precision=highest)
    from_imag = jnp.einsum("mbhi,mhio->mbho", parts[:, 1], mix_weight, precision=highest)
    mixed_real = from_real[..., :head_size] - from_imag[..., head_size:]
    mixed_imag = from_real[..., head_size:] + from_imag[..., :head_size]
    mixed = jnp.stack([mixed_real, mixed_imag], axis=1).astype(jnp.bfloat16)
    mixed = mixed.reshape(2 * own_modes, series_count, group_width)
    mixed = lax.all_gather(mixed, "head", axis=2, tiled=True)
    projected = jnp.einsum("kbf,fo->kbo", mixed, out_weight, preferred_element_type=jnp.float32)
    projected = (projected * inverse_scale).astype(jnp.bfloat16)
    everything = lax.all_gather(projected, "tm", axis=0, tiled=True)
    output = jnp.einsum("tk,kbo->bto", table, everything, preferred_element_type=jnp.float32)
    return output.astype(jnp.bfloat16)


def solution(mesh):
    in_specs = (
        P(None, "tm", None),
        P(),
        P(None, "head"),
        P("tm", "head", None, None),
        P(None, "head"),
    )
    out_specs = P(None, "tm", "head")
    return jax.shard_map(body, mesh=mesh, in_specs=in_specs, out_specs=out_specs, check_vma=False)
```

profile of v0, /device:TPU:0, one launch (start us, length us, event | category | flops | bytes accessed | tf_op | source)
XLA Modules:
  0.0 475.2 jit_solution(6444277786331292956)
XLA Ops:
  6.5 3.2 cosine_convert_fusion
  9.7 0.1 pad_maximum_fusion
  9.8 0.5 copy.30
  10.3 0.2 reshape.141
  10.5 5.7 %fusion.2 = f32[256,8,512]{2,0,1:T(8,128)S(1)} fusion(bf16[1024,256,1]{0,1,2:T(8,128)(2,1)S(1)} %reshape.141, bf16[16,1024,512]{2,1,0:T(8,128)(2,1)} %param.5, s32[]{:T(128)S(6)} %select_n.22), kind=kOutput, calls=%fused_computation.3 | convolution fusion | flops 2148532224 | bytes 13107204 | tf_op jit(solution)/shard_map/tk,btd->kbd/dot_general | solution.py:32
  16.3 4.4 copy.31
  20.7 0.0 reduce-scatter.2.cloned.1.call-update
  20.7 0.0 all-gather.2.cloned.1.call-start
  20.8 360.5 %reduce-scatter.2.cloned.1.call-done = f32[4,8,512]{2,1,0:T(8,128)} async-done(((f32[256,8,512]{2,1,0:T(8,128)}), f32[4,8,512]{2,1,0:T(8,128)}) %reduce-scatter.2.cloned.1.call-update) | async-done | bytes 65552 | tf_op jit(solution)/shard_map/reduce_scatter | solution.py:33
  381.3 0.9 copy.32
  382.2 1.9 all_gather.9
  384.1 0.3 fusion.12
  384.3 0.1 reshape.140
  384.5 0.3 convolution_bitcast_fusion.1
  384.8 0.3 convolution_bitcast_fusion
  385.1 0.1 fusion.17
  385.3 0.1 convert_element_type.36
  385.4 1.8 all_gather.10
  387.3 0.8 fusion.6
  388.1 0.0 all-gather.2.cloned.1.call-update
  388.1 0.2 convert_element_type.35
  388.3 60.4 %all-gather.2.cloned.1.call-done = bf16[256,16,256]{2,1,0:T(8,128)(2,1)} async-done(((bf16[4,16,256]{2,1,0:T(8,128)(2,1)}), bf16[256,16,256]{2,1,0:T(8,128)(2,1)}) %all-gather.2.cloned.1.call-update) | async-done | bytes 2097168 | tf_op jit(solution)/shard_map/all_gather | solution.py:48
  448.7 7.5 %convert_bitcast_fusion = bf16[16,1024,256]{1,2,0:T(8,128)(2,1)} fusion(bf16[256,16,256]{2,1,0:T(8,128)(2,1)} %all-gather.2.cloned.1.call-done, bf16[1024,256]{0,1:T(8,128)(2,1)S(1)} %convert_element_type.35), kind=kOutput, calls=%fused_computation | convolution fusion | flops 2151677952 | bytes 11010048 | tf_op jit(solution)/shard_map/tk,kbo->bto/dot_general | solution.py:49
  456.2 12.2 %copy.39 = bf16[16,1024,256]{2,1,0:T(8,128)(2,1)} copy(bf16[16,1024,256]{1,2,0:T(8,128)(2,1)} %convert_bitcast_fusion) | data formatting | bytes 16777216 | tf_op jit(solution)/shard_map/convert_element_type | solution.py:50
  (11 shorter events, 0.1 us)
Async XLA Ops:
  6.5 377.9 %copy-start = (f32[2,4,64,128]{3,2,1,0:T(8,128)S(1)}, f32[2,4,64,128]{3,2,1,0:T(8,128)}, u32[]{:S(2)}) copy-start(f32[2,4,64,128]{3,2,1,0:T(8,128)} %param.8) | copy-start | bytes 786436
  6.5 374.7 %reduce-scatter.2.cloned.1.call-start = ((), (), s32[]{:S(2)}) async-start(), calls=%async_computation.1 | async-start | bytes 4259840 | tf_op jit(solution)/shard_map/reduce_scatter | solution.py:33
  20.7 363.4 %copy-start.1 = (bf16[512,256]{1,0:T(8,128)(2,1)S(1)}, bf16[512,256]{1,0:T(8,128)(2,1)}, u32[]{:S(2)}) copy-start(bf16[512,256]{1,0:T(8,128)(2,1)} %param.7) | copy-start | bytes 786436
  20.7 366.6 %copy-start.2 = (bf16[512,256]{1,0:T(8,128)(2,1)S(1)}, bf16[512,256]{1,0:T(8,128)(2,1)}, u32[]{:S(2)}) copy-start(bf16[512,256]{1,0:T(8,128)(2,1)} %param.9) | copy-start | bytes 786436
  20.7 428.0 %all-gather.2.cloned.1.call-start = ((), (), s32[]{:S(2)}) async-start(), calls=%async_computation.2 | async-start | bytes 2129920 | tf_op jit(solution)/shard_map/all_gather | solution.py:48
Sparse Core Ops, SparseCore 0:
  20.9 360.3 reduce-scatter.1
  388.2 60.4 all-gather.1
where the time goes:
time: 476 us; the launch traced here: 475 us
  waiting for transfers between devices  421 us (88%)
  local copies, waits for them, and re-layouts  18.7 us (4%)
  matrix products  14.9 us (3%)
  between operations  13.5 us (3%)
    reduce_scatter x1, waiting for transfers between devices, body(): lax.psum_scatter(partial * forward_scale, 'tm', scatter_dimension=0, tile...  360 us
    all_gather x1, waiting for transfers between devices, body(): everything = lax.all_gather(projected, 'tm', axis=0, tiled=True)  60.4 us
    convert_element_type x1, local copies, waits for them, and re-layouts, body(): return output.astype(jnp.bfloat16)  12.2 us
  transfers between devices with their start and end apart: 2, of which 2 were waited for; matrix products, arithmetic and copies ran while one was open for 0% of the time, Pallas kernels for 0%

commit v1 on v0

--- a/solution.py
+++ b/solution.py
@@ -45,7 +45,9 @@
     mixed = lax.all_gather(mixed, "head", axis=2, tiled=True)
     projected = jnp.einsum("kbf,fo->kbo", mixed, out_weight, preferred_element_type=jnp.float32)
     projected = (projected * inverse_scale).astype(jnp.bfloat16)
-    everything = lax.all_gather(projected, "tm", axis=0, tiled=True)
+    everything = jnp.concatenate(
+        lax.all_to_all(jnp.stack([projected] * lax.axis_size("tm")), "tm", 0, 0), axis=0
+    )
     output = jnp.einsum("tk,kbo->bto", table, everything, preferred_element_type=jnp.float32)
     return output.astype(jnp.bfloat16)
 

time: 476 us -> 449 us (0.943)
  waiting for transfers between devices: 421 us -> 390 us
    all_gather x1 -> x0, waiting for transfers between devices: 60.4 us -> none  [body(): everything = lax.all_gather(projected, 'tm', axis=0, tiled=True)]
    all_to_all x0 -> x1, waiting for transfers between devices: none -> 29.9 us  [body(): lax.all_to_all(jnp.stack([projected] * lax.axis_size('tm')), 'tm', 0, 0)]
where the time goes in v1:
time: 449 us
  waiting for transfers between devices  390 us (87%)
  local copies, waits for them, and re-layouts  20.3 us (5%)
  between operations  13.5 us (3%)
  matrix products  12.8 us (3%)
  starting transfers between devices  4.7 us (1%)
    reduce_scatter x1, waiting for transfers between devices, body(): lax.psum_scatter(partial * forward_scale, 'tm', scatter_dimension=0, tile...  361 us
    all_to_all x1, waiting for transfers between devices, body(): lax.all_to_all(jnp.stack([projected] * lax.axis_size('tm')), 'tm', 0, 0)  29.9 us
    convert_element_type x1, local copies, waits for them, and re-layouts, body(): return output.astype(jnp.bfloat16)  12.2 us
  transfers between devices with their start and end apart: 2, of which 2 were waited for; matrix products, arithmetic and copies ran while one was open for 0% of the time, Pallas kernels for 0%

profile of v1, /device:TPU:0, one launch (start us, length us, event | category | flops | bytes accessed | tf_op | source)
XLA Modules:
  0.0 448.9 jit_solution(16668365231518193717)
XLA Ops:
  6.5 3.2 fusion.14
  9.7 0.1 maximum_convert_fusion
  9.8 0.5 copy.24
  10.3 0.2 reshape.154
  10.5 5.7 %fusion.2 = f32[256,8,512]{2,0,1:T(8,128)S(1)} fusion(bf16[1024,256,1]{0,1,2:T(8,128)(2,1)S(1)} %reshape.154, bf16[16,1024,512]{2,1,0:T(8,128)(2,1)} %param.5, s32[]{:T(128)S(6)} %select_n.22), kind=kOutput, calls=%fused_computation.3 | convolution fusion | flops 2148532224 | bytes 13107204 | tf_op jit(solution)/shard_map/tk,btd->kbd/dot_general | solution.py:32
  16.3 4.4 copy.25
  20.7 0.0 reduce-scatter.2.cloned.1.call-update
  20.7 360.5 %reduce-scatter.2.cloned.1.call-done = f32[4,8,512]{2,1,0:T(8,128)} async-done(((f32[256,8,512]{2,1,0:T(8,128)}), f32[4,8,512]{2,1,0:T(8,128)}) %reduce-scatter.2.cloned.1.call-update) | async-done | bytes 65552 | tf_op jit(solution)/shard_map/reduce_scatter | solution.py:33
  381.3 0.9 copy.26
  382.2 1.9 all_gather.6
  384.1 0.3 fusion.12
  384.3 0.1 reshape.152
  384.5 0.3 convolution_bitcast_fusion.1
  384.8 0.3 convolution_bitcast_fusion
  385.1 0.1 fusion.18
  385.3 0.1 convert_element_type.46
  385.4 1.8 all_gather.7
  387.3 0.2 fusion.6
  387.4 1.6 stack.17
  389.0 4.7 %all-to-all-start = ((bf16[64,4,16,256]{3,2,1,0:T(8,128)(2,1)}), bf16[64,4,16,256]{3,2,1,0:T(8,128)(2,1)S(1)}, u32[]{:S(2)}, u32[]{:S(2)}) async-start(bf16[64,4,16,256]{3,2,1,0:T(8,128)(2,1)} %stack.17), calls=%async_computation.1 | async-start | bytes 4194304 | tf_op jit(solution)/shard_map/all_to_all | solution.py:49
  393.7 0.2 convert_element_type.45
  393.9 29.9 %all-to-all-done = bf16[64,4,16,256]{3,2,1,0:T(8,128)(2,1)S(1)} async-done(((bf16[64,4,16,256]{3,2,1,0:T(8,128)(2,1)}), bf16[64,4,16,256]{3,2,1,0:T(8,128)(2,1)S(1)}, u32[]{:S(2)}, u32[]{:S(2)}) %all-to-all-start) | async-done | bytes 2097184 | tf_op jit(solution)/shard_map/all_to_all | solution.py:49
  423.8 6.0 %convert_bitcast_fusion = bf16[16,1024,256]{1,2,0:T(8,128)(2,1)} fusion(bf16[256,16,256]{2,1,0:T(8,128)(2,1)S(1)} %bitcast.34, bf16[1024,256]{0,1:T(8,128)(2,1)S(1)} %convert_element_type.45), kind=kOutput, calls=%fused_computation | convolution fusion | flops 2151677952 | bytes 11010048 | tf_op jit(solution)/shard_map/tk,kbo->bto/dot_general | solution.py:51
  429.8 12.2 %copy.33 = bf16[16,1024,256]{2,1,0:T(8,128)(2,1)} copy(bf16[16,1024,256]{1,2,0:T(8,128)(2,1)} %convert_bitcast_fusion) | data formatting | bytes 16777216 | tf_op jit(solution)/shard_map/convert_element_type | solution.py:52
  (11 shorter events, 0.1 us)
Async XLA Ops:
  6.5 377.9 %copy-start = (f32[2,4,64,128]{3,2,1,0:T(8,128)S(1)}, f32[2,4,64,128]{3,2,1,0:T(8,128)}, u32[]{:S(2)}) copy-start(f32[2,4,64,128]{3,2,1,0:T(8,128)} %param.8) | copy-start | bytes 786436
  6.5 374.7 %reduce-scatter.2.cloned.1.call-start = ((), (), s32[]{:S(2)}) async-start(), calls=%async_computation.2 | async-start | bytes 4259840 | tf_op jit(solution)/shard_map/reduce_scatter | solution.py:33
  20.7 363.4 %copy-start.1 = (bf16[512,256]{1,0:T(8,128)(2,1)S(1)}, bf16[512,256]{1,0:T(8,128)(2,1)}, u32[]{:S(2)}) copy-start(bf16[512,256]{1,0:T(8,128)(2,1)} %param.7) | copy-start | bytes 786436
  20.7 366.6 %copy-start.2 = (bf16[512,256]{1,0:T(8,128)(2,1)S(1)}, bf16[512,256]{1,0:T(8,128)(2,1)}, u32[]{:S(2)}) copy-start(bf16[512,256]{1,0:T(8,128)(2,1)} %param.9) | copy-start | bytes 786436
  389.0 34.8 %all-to-all-start = ((bf16[64,4,16,256]{3,2,1,0:T(8,128)(2,1)}), bf16[64,4,16,256]{3,2,1,0:T(8,128)(2,1)S(1)}, u32[]{:S(2)}, u32[]{:S(2)}) async-start(bf16[64,4,16,256]{3,2,1,0:T(8,128)(2,1)} %stack.17), calls=%async_computation.1 | async-start | bytes 4194304 | tf_op jit(solution)/shard_map/all_to_all | solution.py:49
Sparse Core Ops, SparseCore 0:
  20.9 360.3 reduce-scatter.1
